TPU v7x, 512 devices: a whole 4x8x8 slice. The times are simulated.
512 devices in a mesh: dp: 128 (over y, z, core), feat: 4 (over x).
Axes of the slice: x: 4, y: 8, z: 8, core: 2. Of those that a mesh axis runs over, the one named last changes fastest.
Arguments:
- activations: bfloat16 [131072, 8192], P('dp', 'feat'), may hold values from -6 to 6
- cand_index: int32 [131072], P('dp'), may hold values from 0 to 127
- labels: int32 [8192], P('dp'), may hold values 0 or 1
- counts: int32 [128], P('dp'), may hold values from 1 to 64, as said below
Outputs:
- scores: float32 [131072, 128], P('dp', 'feat')
Inputs may be any that keep to these rules, and one draw needn't show every extreme that they name: `counts`: the fullest slab has all 64 prompt slots live.
All inputs are finite; a program needn't handle non-finite values. No bound on the sum of `labels` on one device may be relied on, other than what follows from the above.
Results may differ from a plain program's by a relative error of at most 0.0047.
Values may be sent and summed in bfloat16 or wider, within the bound.
A program may use at most 64 MiB of HBM per device.

v0:
```python
import jax
import jax.numpy as jnp
from jax import lax
from jax.sharding import PartitionSpec as P

CAND_DEV = 1
PER_PROMPT = 16
epsilon = 1e-06


def project(activations, dir_block):
    return lax.dot_general(
        activations, dir_block, (((1,), (1,)), ((), ())), preferred_element_type=jnp.float32
    )


def per_device(activations, cand_index, labels, counts):
    row_total = activations.shape[0]
    cand_total = CAND_DEV * lax.axis_size("dp")
    prompt_of = jnp.arange(row_total, dtype=jnp.int32) // PER_PROMPT
    live = prompt_of < counts[0]
    classes = jnp.repeat(labels, PER_PROMPT)
    cand_ids = jnp.arange(cand_total, dtype=jnp.int32)
    matches = (cand_index[None, :] == cand_ids[:, None]) & live[None, :]
    harmful_hits = matches & (classes[None, :] == 1)
    harmless_hits = matches & (classes[None, :] == 0)
    member = jnp.concatenate([harmful_hits, harmless_hits], axis=0).astype(jnp.bfloat16)
    class_sums = jnp.dot(member, activations, preferred_element_type=jnp.float32).reshape(
        2, cand_total, -1
    )
    class_counts = jnp.sum(member.astype(jnp.float32), axis=1).reshape(2, cand_total)
    owned_sums, owned_counts = (
        lax.psum_scatter(class_sums, "dp", scatter_dimension=1, tiled=True),
        lax.psum_scatter(class_counts, "dp", scatter_dimension=1, tiled=True),
    )
    harmful_mean = owned_sums[0] / jnp.maximum(owned_counts[0], 1.0)[:, None]
    harmless_mean = owned_sums[1] / jnp.maximum(owned_counts[1], 1.0)[:, None]
    raw_float = harmful_mean - harmless_mean
    raw_dir = raw_float.astype(jnp.bfloat16)
    squares = jnp.sum(jnp.square(raw_dir.astype(jnp.float32)), axis=1)
    total_sq = lax.psum(squares, "feat")
    inv_norm = lax.rsqrt(total_sq + epsilon).astype(jnp.bfloat16)
    dir_block = lax.all_gather(raw_dir, "dp", axis=0, tiled=True)
    inv_block = lax.all_gather(inv_norm, "dp", axis=0, tiled=True)
    partial_value = project(activations, dir_block) * inv_block.astype(jnp.float32)[None, :]
    return lax.psum_scatter(partial_value, "feat", scatter_dimension=1, tiled=True)


def solution(mesh):
    return jax.shard_map(
        per_device,
        mesh=mesh,
        in_specs=(P("dp", "feat"), P("dp"), P("dp"), P("dp")),
        out_specs=P("dp", "feat"),
        check_vma=False,
    )
```

profile of v0, /device:TPU:8, one launch (start us, length us, event | category | flops | bytes accessed | tf_op | source)
XLA Modules:
  0.0 619.2 jit_solution(13851311557933916579)
XLA Ops:
  6.5 0.0 all-reduce.5.cloned.1.call-start
  6.5 0.7 broadcast_compare_fusion.1
  7.2 0.1 broadcast_in_dim.4
  7.3 0.1 eq.43
  7.4 0.1 broadcast_in_dim.5
  7.4 0.1 eq.45
  8.2 0.9 fusion.5
  9.1 3.4 fusion.6
  12.5 0.0 copy-start
  12.5 2.9 copy.8
  15.5 0.0 all-reduce.5.cloned.1.call-update
  15.5 0.0 reduce-scatter.3.cloned.1.call-start
  15.5 0.0 copy-done
  15.5 0.6 fusion.12
  16.1 0.2 convert_reduce_fusion
  16.3 222.9 %all-reduce.2 = f32[2,128]{1,0:T(2,128)S(1)} all-reduce(f32[2,128]{1,0:T(2,128)S(1)} %bitcast.23), channel_id=4, replica_groups=mesh['dp'=128,'feat'=4] {'dp'}, use_global_device_ids=true, to_apply=%region_2.3.clone | all-reduce | flops 256 | bytes 2048
  239.2 0.7 constant_dynamic-slice_fusion
  239.9 0.6 fusion.13
  241.8 0.0 all-reduce.5.cloned.1.call-done
  241.8 2.0 multiply_reduce_fusion
  243.9 11.3 %psum.7 = f32[1]{0:T(128)} all-reduce(f32[1]{0:T(128)} %bitcast.6), channel_id=1, replica_groups=mesh['dp'=128,'feat'=4] {'feat'}, use_global_device_ids=true, to_apply=%region_4.5 | all-reduce | flops 1 | bytes 8 | tf_op jit(solution)/shard_map/psum | solution.py:41
  256.4 1.3 dynamic-update-slice
  257.7 247.1 %all-reduce = bf16[128]{0:T(256)(128)(2,1)S(1)} all-reduce(bf16[128]{0:T(256)(128)(2,1)S(1)} %dynamic-update-slice), channel_id=1, replica_groups=mesh['dp'=128,'feat'=4] {'dp'}, use_global_device_ids=true, to_apply=%add | all-reduce | flops 128 | bytes 512
  504.8 83.2 %all-gather = bf16[128,1,2048]{2,1,0:T(2,128)(2,1)S(1)} all-gather(bf16[1,1,2048]{2,1,0:T(2,128)(2,1)S(1)} %bitcast.22), channel_id=2, replica_groups=mesh['dp'=128,'feat'=4] {'dp'}, dimensions={0}, use_global_device_ids=true | all-gather | bytes 528384 | tf_op jit(solution)/shard_map/all_gather | solution.py:43
  588.0 4.6 fusion
  592.5 0.0 reduce-scatter.3.cloned.1.call-update
  592.5 19.8 %reduce-scatter.3.cloned.1.call-done = f32[1024,32]{0,1:T(8,128)} async-done(((f32[1024,128]{0,1:T(8,128)}), f32[1024,32]{0,1:T(8,128)}) %reduce-scatter.3.cloned.1.call-update) | async-done | bytes 131088 | tf_op jit(solution)/shard_map/reduce_scatter | solution.py:46
  (3 shorter events, 0.0 us)
Async XLA Ops:
  6.5 235.3 %all-reduce.5.cloned.1.call-start = ((), (), s32[]{:S(2)}) async-start(), calls=%async_computation.2 | async-start | bytes 4194304
  12.5 3.0 copy-start
  15.5 596.9 %reduce-scatter.3.cloned.1.call-start = ((), (), s32[]{:S(2)}) async-start(), calls=%async_computation.1 | async-start | bytes 655360 | tf_op jit(solution)/shard_map/reduce_scatter | solution.py:46
Sparse Core Ops, SparseCore 0:
  15.6 204.9 all-reduce.4
  592.7 19.6 reduce-scatter.2
where the time goes:
time: 620 us; the launch traced here: 619 us
  blocking collectives  564 us (91%)
  waiting for transfers between devices  19.9 us (3%)
  between operations  16.6 us (3%)
  matrix products  8.01 us (1%)
  local copies, waits for them, and re-layouts  6.46 us (1%)
    unnamed x2, blocking collectives  470 us
    all_gather x1, blocking collectives, per_device(): dir_block = lax.all_gather(raw_dir, 'dp', axis=0, tiled=True)  83.2 us
    reduce_scatter x1, waiting for transfers between devices, per_device(): lax.psum_scatter(partial_value, 'feat', scatter_dimension=1, tiled=True)  19.8 us
  transfers between devices with their start and end apart: 2, of which 1 were waited for; matrix products, arithmetic and copies ran while one was open for 0% of the time, Pallas kernels for 0%

commit v1 on v0

--- a/solution.py
+++ b/solution.py
@@ -40,7 +40,10 @@
     squares = jnp.sum(jnp.square(raw_dir.astype(jnp.float32)), axis=1)
     total_sq = lax.psum(squares, "feat")
     inv_norm = lax.rsqrt(total_sq + epsilon).astype(jnp.bfloat16)
-    dir_block = lax.all_gather(raw_dir, "dp", axis=0, tiled=True)
+    state_next = lax.axis_size("dp")
+    n_now = jnp.stack([raw_dir] * state_next)
+    kept_arr = lax.all_to_all(n_now, axis_name="dp", split_axis=0, concat_axis=0)
+    dir_block = jnp.concatenate(kept_arr, 0)
     inv_block = lax.all_gather(inv_norm, "dp", axis=0, tiled=True)
     partial_value = project(activations, dir_block) * inv_block.astype(jnp.float32)[None, :]
     return lax.psum_scatter(partial_value, "feat", scatter_dimension=1, tiled=True)

time: 620 us -> 586 us (0.945)
  blocking collectives: 564 us -> 450 us
  starting transfers between devices: 0.04 us -> 41.4 us
  waiting for transfers between devices: 19.9 us -> 53.3 us
    all_gather x1 -> x0, blocking collectives: 83.2 us -> none  [per_device(): dir_block = lax.all_gather(raw_dir, 'dp', axis=0, tiled=True)]
    all_to_all x0 -> x1, starting transfers between devices: none -> 41.3 us  [per_device(): lax.all_to_all(n_now, axis_name='dp', split_axis=0, concat_axis=0)]
    reduce_scatter x1, waiting for transfers between devices: 19.8 us -> 53.3 us  [per_device(): lax.psum_scatter(partial_value, 'feat', scatter_dimension=1, tiled=True)]
    unnamed x2, blocking collectives: 470 us -> 438 us
  transfers between devices with their start and end apart: 2 -> 3, of which waited for: 1 -> 1; matrix products, arithmetic and copies ran while one was open for 0% -> 1% of each run, Pallas kernels for 0% -> 0%
where the time goes in v1:
time: 586 us
  blocking collectives  450 us (77%)
  waiting for transfers between devices  53.3 us (9%)
  starting transfers between devices  41.4 us (7%)
  between operations  16.6 us (3%)
  local copies, waits for them, and re-layouts  9.26 us (2%)
  matrix products  7.97 us (1%)
  other arithmetic  7.5 us (1%)
    unnamed x2, blocking collectives  438 us
    reduce_scatter x1, waiting for transfers between devices, per_device(): lax.psum_scatter(partial_value, 'feat', scatter_dimension=1, tiled=True)  53.3 us
    all_to_all x1, starting transfers between devices, per_device(): lax.all_to_all(n_now, axis_name='dp', split_axis=0, concat_axis=0)  41.3 us
  transfers between devices with their start and end apart: 3, of which 1 were waited for; matrix products, arithmetic and copies ran while one was open for 1% of the time, Pallas kernels for 0%

profile of v1, /device:TPU:8, one launch (start us, length us, event | category | flops | bytes accessed | tf_op | source)
XLA Modules:
  0.0 585.6 jit_solution(10711074382660551600)
XLA Ops:
  6.5 0.0 all-reduce.5.cloned.1.call-start
  6.5 0.7 broadcast_compare_fusion.1
  7.2 0.1 broadcast_in_dim.4
  7.3 0.1 eq.43
  7.4 0.1 broadcast_in_dim.5
  7.4 0.1 eq.45
  8.2 0.9 fusion.5
  9.1 3.4 fusion.6
  12.5 0.0 copy-start
  12.5 2.9 copy.6
  15.5 0.0 all-reduce.5.cloned.1.call-update
  15.5 0.0 copy-done
  15.5 0.6 fusion.12
  16.1 0.2 convert_reduce_fusion
  16.3 222.8 %all-reduce.2 = f32[2,128]{1,0:T(2,128)S(1)} all-reduce(f32[2,128]{1,0:T(2,128)S(1)} %bitcast.19), channel_id=3, replica_groups=mesh['dp'=128,'feat'=4] {'dp'}, use_global_device_ids=true, to_apply=%region_2.3.clone | all-reduce | flops 256 | bytes 2048
  239.1 0.7 constant_dynamic-slice_fusion
  239.7 0.6 fusion.13
  241.6 0.0 all-reduce.5.cloned.1.call-done
  241.6 2.0 multiply_reduce_fusion
  243.7 0.5 stack.5
  244.3 0.6 broadcast.88
  244.9 3.7 reduce.4
  248.6 1.2 reshape.124
  249.8 41.3 %all-to-all-start = ((bf16[128,2,1024]{2,1,0:T(2,128)(2,1)}), bf16[128,2,1024]{2,1,0:T(2,128)(2,1)S(1)}, u32[]{:S(2)}, u32[]{:S(2)}) async-start(bf16[128,2,1024]{2,1,0:T(2,128)(2,1)} %reshape.124), calls=%async_computation | async-start | bytes 1048576 | tf_op jit(solution)/shard_map/all_to_all | solution.py:45
  291.1 0.0 reduce-scatter.3.cloned.1.call-start
  291.2 11.2 %psum.7 = f32[1]{0:T(128)} all-reduce(f32[1]{0:T(128)} %bitcast.5), channel_id=1, replica_groups=mesh['dp'=128,'feat'=4] {'feat'}, use_global_device_ids=true, to_apply=%region_4.5 | all-reduce | flops 1 | bytes 8 | tf_op jit(solution)/shard_map/psum | solution.py:41
  303.6 1.3 dynamic-update-slice
  304.9 215.6 %all-reduce = bf16[128]{0:T(256)(128)(2,1)S(1)} all-reduce(bf16[128]{0:T(256)(128)(2,1)S(1)} %dynamic-update-slice), channel_id=1, replica_groups=mesh['dp'=128,'feat'=4] {'dp'}, use_global_device_ids=true, to_apply=%add | all-reduce | flops 128 | bytes 512
  520.4 0.0 all-to-all-done
  520.5 0.5 reshape.125
  520.9 4.5 fusion
  525.4 0.0 reduce-scatter.3.cloned.1.call-update
  525.5 53.3 %reduce-scatter.3.cloned.1.call-done = f32[1024,32]{0,1:T(8,128)} async-done(((f32[1024,128]{0,1:T(8,128)}), f32[1024,32]{0,1:T(8,128)}) %reduce-scatter.3.cloned.1.call-update) | async-done | bytes 131088 | tf_op jit(solution)/shard_map/reduce_scatter | solution.py:49
  (4 shorter events, 0.1 us)
Async XLA Ops:
  6.5 235.1 %all-reduce.5.cloned.1.call-start = ((), (), s32[]{:S(2)}) async-start(), calls=%async_computation.3 | async-start | bytes 4194304
  12.5 3.0 copy-start
  249.8 270.7 %all-to-all-start = ((bf16[128,2,1024]{2,1,0:T(2,128)(2,1)}), bf16[128,2,1024]{2,1,0:T(2,128)(2,1)S(1)}, u32[]{:S(2)}, u32[]{:S(2)}) async-start(bf16[128,2,1024]{2,1,0:T(2,128)(2,1)} %reshape.124), calls=%async_computation | async-start | bytes 1048576 | tf_op jit(solution)/shard_map/all_to_all | solution.py:45
  291.1 287.6 %reduce-scatter.3.cloned.1.call-start = ((), (), s32[]{:S(2)}) async-start(), calls=%async_computation.2 | async-start | bytes 655360 | tf_op jit(solution)/shard_map/reduce_scatter | solution.py:49
Sparse Core Ops, SparseCore 0:
  15.6 204.6 all-reduce.4
  525.6 53.1 reduce-scatter.2
